TPU v7x, 128 devices: a whole 4x4x4 slice. The times are simulated.
128 devices in a mesh: wide: 32 (over x, z, core), narrow: 4 (over y).
Axes of the slice: x: 4, y: 4, z: 4, core: 2. Of those that a mesh axis runs over, the one named last changes fastest.
Arguments:
- front: bfloat16 [4, 32, 128, 32, 4, 128], P(None, 'wide', None, None, 'narrow'), may hold values from -6 to 6
- pivot_inverse: bfloat16 [4, 128, 128], replicated, may hold values from -0.0105112052 to 0.17838107
- rhs: bfloat16 [4, 32, 128, 256], P(None, 'wide'), may hold values from -6 to 6
- trail_sol: bfloat16 [4, 32, 128, 256], P(None, 'wide'), may hold values from -1.1953125 to 1.1953125
- block_mask: int32 [4, 32, 32, 4], P(None, 'wide', None, 'narrow'), may hold values 0 or 1
- panel_order: int32 [4], replicated, may hold values from 0 to 3, each once
Outputs:
- front_out: bfloat16 [4, 32, 128, 32, 4, 128], P(None, 'wide', None, None, 'narrow')
- forward_rhs: bfloat16 [4, 32, 128, 256], P(None, 'wide')
- window_solution: bfloat16 [4, 128, 256], replicated
Inputs may be any that keep to these rules, and one draw needn't show every extreme that they name: `panel_order`: each value 0 to 3 appears once.
All inputs are finite; a program needn't handle non-finite values. No bound on the sum of `block_mask` on one device may be relied on, other than what follows from the above.
Results may differ from a plain program's by a relative error of at most 0.0076.
Values may be sent and summed in bfloat16 or wider, within the bound.
No kernel may reach another device: no remote copies, remote signals or barrier semaphores. Data moves between devices by JAX's collectives and lax.ppermute only.
A program may use at most 64 MiB of HBM per device.

v0:
```python
import jax
import jax.numpy as jnp
from jax import lax
from jax.sharding import PartitionSpec as P


def spread(block, axis, source):
    block = jnp.where(lax.axis_index(axis) == source, block, jnp.zeros_like(block))
    return lax.psum(block, axis)


def body(front, pivot_inverse, rhs, trail_sol, block_mask, panel_order):
    rloc = front.shape[0]
    bsize = front.shape[2]
    cloc = front.shape[3]
    nrhs_local = rhs.shape[3]
    panels = panel_order.shape[0]
    nwide = lax.axis_size("wide")
    nnarrow = lax.axis_size("narrow")
    blocks = front.reshape(rloc, bsize, cloc, bsize)
    pattern = block_mask.reshape(rloc, cloc).astype(jnp.float32)
    right = rhs.reshape(rloc, bsize, nrhs_local)
    rows_global = jnp.arange(rloc, dtype=jnp.int32) * nwide + lax.axis_index("wide")
    cols_global = jnp.arange(cloc, dtype=jnp.int32) * nnarrow + lax.axis_index("narrow")
    section_ids = jnp.arange(panels, dtype=jnp.int32)
    rows_rank = jnp.min(
        jnp.where(rows_global[:, None] == panel_order[None, :], section_ids[None, :], panels),
        axis=1,
    )
    cols_rank = jnp.min(
        jnp.where(cols_global[:, None] == panel_order[None, :], section_ids[None, :], panels),
        axis=1,
    )

    def pivot_weight(target):
        return lax.dynamic_index_in_dim(pivot_inverse, target, 0, keepdims=False)

    def panel_factors(col_blocks, row_blocks, target, section):
        weight = pivot_weight(target)
        left = jnp.einsum("rab,bc->rac", col_blocks, weight, preferred_element_type=jnp.float32)
        left = jnp.where((rows_rank > section)[:, None, None], left, 0.0).astype(jnp.bfloat16)
        left = spread(left, "narrow", target % nnarrow)
        upper = jnp.einsum("ac,ajb->cjb", weight, row_blocks, preferred_element_type=jnp.float32)
        upper = jnp.where((cols_rank > section)[None, :, None], upper, 0.0).astype(jnp.bfloat16)
        upper = spread(upper, "wide", target % nwide)
        return (left, upper)

    def column_of(current, target):
        return lax.dynamic_index_in_dim(current, target // nnarrow, 2, keepdims=False)

    def row_of(current, target):
        return lax.dynamic_index_in_dim(current, target // nwide, 0, keepdims=False)

    saved_left = []
    saved_pivot = []
    left, upper = panel_factors(
        column_of(blocks, panel_order[0]), row_of(blocks, panel_order[0]), panel_order[0], 0
    )
    for section in range(panels):
        target = panel_order[section]
        weight = pivot_weight(target)
        product = jnp.einsum("rac,cjb->rajb", left, upper, preferred_element_type=jnp.float32)
        blocks = (blocks.astype(jnp.float32) - pattern[:, None, :, None] * product).astype(
            jnp.bfloat16
        )
        if section + 1 < panels:
            following = panel_order[section + 1]
            next_left, next_upper = panel_factors(
                column_of(blocks, following), row_of(blocks, following), following, section + 1
            )
        pivot_rhs = lax.dynamic_index_in_dim(right, target // nwide, 0, keepdims=False)
        solved = jnp.einsum(
            "ac,an->cn", weight, pivot_rhs, preferred_element_type=jnp.float32
        ).astype(jnp.bfloat16)
        solved = spread(solved, "wide", target % nwide)
        elimination = jnp.einsum("rac,cn->ran", left, solved, preferred_element_type=jnp.float32)
        right = (right.astype(jnp.float32) - elimination).astype(jnp.bfloat16)
        saved_left.append(left)
        saved_pivot.append(solved)
        if section + 1 < panels:
            left, upper = (next_left, next_upper)
    current = trail_sol.reshape(rloc, bsize, nrhs_local)
    window = jnp.zeros((panels, bsize, nrhs_local), jnp.bfloat16)
    for section in reversed(range(panels)):
        target = panel_order[section]
        partial_sum = jnp.einsum(
            "rac,ran->cn", saved_left[section], current, preferred_element_type=jnp.float32
        )
        total = lax.psum(partial_sum, "wide")
        corrected = (saved_pivot[section].astype(jnp.float32) - total).astype(jnp.bfloat16)
        result = jnp.einsum(
            "ac,cn->an", pivot_weight(target), corrected, preferred_element_type=jnp.float32
        ).astype(jnp.bfloat16)
        current = jnp.where((rows_global == target)[:, None, None], result[None], current)
        window = lax.dynamic_update_index_in_dim(window, result, target, 0)
    return (blocks.reshape(front.shape), right.reshape(rhs.shape), window)


def solution(mesh):
    in_specs = (
        P(None, "wide", None, None, "narrow", None),
        P(),
        P(None, "wide", None, None),
        P(None, "wide", None, None),
        P(None, "wide", None, "narrow"),
        P(),
    )
    out_specs = (P(None, "wide", None, None, "narrow", None), P(None, "wide", None, None), P())
    return jax.shard_map(body, mesh=mesh, in_specs=in_specs, out_specs=out_specs, check_vma=False)
```

profile of v0, /device:TPU:1, one launch (start us, length us, event | category | flops | bytes accessed | tf_op | source)
XLA Modules:
  0.0 1070.7 jit_solution(9461470469571352421)
XLA Ops:
  7.2 1.5 fusion.111
  13.5 1.5 constant_dynamic-slice_fusion.1
  16.0 1.3 constant_dynamic-slice_fusion
  18.1 1.6 fusion.2
  24.1 34.5 %all-reduce.17.cloned.1.call-done = bf16[4,128,128]{2,1,0:T(8,128)(2,1)} async-done(((bf16[4,128,128]{2,1,0:T(8,128)(2,1)}), bf16[4,128,128]{2,1,0:T(8,128)(2,1)}) %all-reduce.17.cloned.1.call-update) | async-done | bytes 131088 | tf_op jit(solution)/shard_map/psum | solution.py:9
  58.6 112.0 %all-reduce.39.cloned.1.call-done = (bf16[128,32,128]{2,0,1:T(8,128)(2,1)}, bf16[128,256]{1,0:T(8,128)(2,1)}) async-done(((bf16[128,32,128]{2,0,1:T(8,128)(2,1)}, bf16[128,256]{1,0:T(8,128)(2,1)}), (bf16[128,32,128]{2,0,1:T(8,128)(2,1)}, bf16[128,256]{1,0:T(8,128)(2,1)})) %all-reduce.39.cloned.1.call-update) | async-done | bytes 1114128 | tf_op jit(solution)/shard_map/psum | solution.py:9
  170.6 4.7 fusion
  175.3 2.0 copy-done.2
  178.2 2.7 fusion.3
  185.6 31.7 %all-reduce.19.cloned.1.call-done = bf16[4,128,128]{2,1,0:T(8,128)(2,1)} async-done(((bf16[4,128,128]{2,1,0:T(8,128)(2,1)}), bf16[4,128,128]{2,1,0:T(8,128)(2,1)}) %all-reduce.19.cloned.1.call-update) | async-done | bytes 131088 | tf_op jit(solution)/shard_map/psum | solution.py:9
  217.3 111.8 %all-reduce.37.cloned.1.call-done = (bf16[128,32,128]{2,0,1:T(8,128)(2,1)}, bf16[128,256]{1,0:T(8,128)(2,1)}) async-done(((bf16[128,32,128]{2,0,1:T(8,128)(2,1)}, bf16[128,256]{1,0:T(8,128)(2,1)}), (bf16[128,32,128]{2,0,1:T(8,128)(2,1)}, bf16[128,256]{1,0:T(8,128)(2,1)})) %all-reduce.37.cloned.1.call-update) | async-done | bytes 1114128 | tf_op jit(solution)/shard_map/psum | solution.py:9
  329.1 3.8 subtract_convert_fusion.2
  333.0 2.0 copy-done.1
  335.9 2.7 fusion.4
  343.9 31.0 %all-reduce.21.cloned.1.call-done = bf16[4,128,128]{2,1,0:T(8,128)(2,1)} async-done(((bf16[4,128,128]{2,1,0:T(8,128)(2,1)}), bf16[4,128,128]{2,1,0:T(8,128)(2,1)}) %all-reduce.21.cloned.1.call-update) | async-done | bytes 131088 | tf_op jit(solution)/shard_map/psum | solution.py:9
  374.9 111.8 %all-reduce.35.cloned.1.call-done = (bf16[128,32,128]{2,0,1:T(8,128)(2,1)}, bf16[128,256]{1,0:T(8,128)(2,1)}) async-done(((bf16[128,32,128]{2,0,1:T(8,128)(2,1)}, bf16[128,256]{1,0:T(8,128)(2,1)}), (bf16[128,32,128]{2,0,1:T(8,128)(2,1)}, bf16[128,256]{1,0:T(8,128)(2,1)})) %all-reduce.35.cloned.1.call-update) | async-done | bytes 1114128 | tf_op jit(solution)/shard_map/psum | solution.py:9
  486.7 3.8 subtract_convert_fusion.1
  490.6 2.0 copy-done.3
  493.5 2.7 fusion.5
  496.4 36.1 %all-reduce.23.cloned.1.call-done = bf16[4,128,128]{2,1,0:T(8,128)(2,1)} async-done(((bf16[4,128,128]{2,1,0:T(8,128)(2,1)}), bf16[4,128,128]{2,1,0:T(8,128)(2,1)}) %all-reduce.23.cloned.1.call-update) | async-done | bytes 131088 | tf_op jit(solution)/shard_map/psum | solution.py:9
  532.5 1.9 convolution_bitcast_fusion.3
  536.7 103.3 %all-reduce.25.cloned.1.call-done = f32[128,256]{1,0:T(8,128)} async-done(((f32[128,256]{1,0:T(8,128)}), f32[128,256]{1,0:T(8,128)}) %all-reduce.25.cloned.1.call-update) | async-done | bytes 131088 | tf_op jit(solution)/shard_map/psum | solution.py:89
  639.9 109.0 %all-reduce.33.cloned.1.call-done = (bf16[128,32,128]{2,0,1:T(8,128)(2,1)}, bf16[128,256]{1,0:T(8,128)(2,1)}) async-done(((bf16[128,32,128]{2,0,1:T(8,128)(2,1)}, bf16[128,256]{1,0:T(8,128)(2,1)}), (bf16[128,32,128]{2,0,1:T(8,128)(2,1)}, bf16[128,256]{1,0:T(8,128)(2,1)})) %all-reduce.33.cloned.1.call-update) | async-done | bytes 1114128 | tf_op jit(solution)/shard_map/psum | solution.py:9
  749.0 1.1 bitcast_dynamic-update-slice_fusion.2
  751.6 101.7 %all-reduce.27.cloned.1.call-done = f32[128,256]{1,0:T(8,128)} async-done(((f32[128,256]{1,0:T(8,128)}), f32[128,256]{1,0:T(8,128)}) %all-reduce.27.cloned.1.call-update) | async-done | bytes 131088 | tf_op jit(solution)/shard_map/psum | solution.py:89
  853.3 1.1 bitcast_dynamic-update-slice_fusion.1
  855.5 5.7 fusion.1
  861.3 96.5 %all-reduce.29.cloned.1.call-done = f32[128,256]{1,0:T(8,128)} async-done(((f32[128,256]{1,0:T(8,128)}), f32[128,256]{1,0:T(8,128)}) %all-reduce.29.cloned.1.call-update) | async-done | bytes 131088 | tf_op jit(solution)/shard_map/psum | solution.py:89
  957.7 1.1 bitcast_dynamic-update-slice_fusion
  960.7 6.9 copy.30
  967.6 94.5 %all-reduce.31.cloned.1.call-done = f32[128,256]{1,0:T(8,128)} async-done(((f32[128,256]{1,0:T(8,128)}), f32[128,256]{1,0:T(8,128)}) %all-reduce.31.cloned.1.call-update) | async-done | bytes 131088 | tf_op jit(solution)/shard_map/psum | solution.py:89
  1062.1 1.0 fusion.24
  (79 shorter events, 16.1 us)
Async XLA Ops:
  7.2 7.9 copy-start
  7.2 12.5 %copy-start.9 = (bf16[4,1,128,256]{3,2,1,0:T(8,128)(2,1)S(1)}, bf16[4,1,128,256]{3,2,1,0:T(8,128)(2,1)}, u32[]{:S(2)}) copy-start(bf16[4,1,128,256]{3,2,1,0:T(8,128)(2,1)} %param.8) | copy-start | bytes 786436
  7.2 16.3 %copy-start.15 = (s32[4,1,32,1]{2,3,1,0:T(1,128)S(1)}, s32[4,1,32,1]{2,3,1,0:T(1,128)}, u32[]{:S(2)}) copy-start(s32[4,1,32,1]{2,3,1,0:T(1,128)} %param.10) | copy-start | bytes 1540
  7.2 51.4 %all-reduce.17.cloned.1.call-start = ((), (), s32[]{:S(2)}) async-start(), calls=%async_computation | async-start | bytes 262144 | tf_op jit(solution)/shard_map/psum | solution.py:9
  15.9 154.7 %all-reduce.39.cloned.1.call-start = ((), (), s32[]{:S(2)}) async-start(), calls=%async_computation.11 | async-start | bytes 2228224 | tf_op jit(solution)/shard_map/psum | solution.py:9
  20.5 196.7 %all-reduce.19.cloned.1.call-start = ((), (), s32[]{:S(2)}) async-start(), calls=%async_computation.1 | async-start | bytes 262144 | tf_op jit(solution)/shard_map/psum | solution.py:9
  170.6 10.3 copy-start.7
  170.6 10.3 copy-start.11
  175.3 2.0 copy-start.2
  178.2 150.9 %all-reduce.37.cloned.1.call-start = ((), (), s32[]{:S(2)}) async-start(), calls=%async_computation.10 | async-start | bytes 2228224 | tf_op jit(solution)/shard_map/psum | solution.py:9
  182.0 192.9 %all-reduce.21.cloned.1.call-start = ((), (), s32[]{:S(2)}) async-start(), calls=%async_computation.2 | async-start | bytes 262144 | tf_op jit(solution)/shard_map/psum | solution.py:9
  329.1 9.5 copy-start.8
  329.1 9.5 copy-start.12
  333.0 2.0 copy-start.1
  335.8 150.9 %all-reduce.35.cloned.1.call-start = ((), (), s32[]{:S(2)}) async-start(), calls=%async_computation.9 | async-start | bytes 2228224 | tf_op jit(solution)/shard_map/psum | solution.py:9
  339.6 192.9 %all-reduce.23.cloned.1.call-start = ((), (), s32[]{:S(2)}) async-start(), calls=%async_computation.3 | async-start | bytes 262144 | tf_op jit(solution)/shard_map/psum | solution.py:9
  486.7 9.5 copy-start.4
  486.7 9.5 copy-start.13
  486.7 45.8 %copy-start.6 = (bf16[4,1,128,256]{3,2,1,0:T(8,128)(2,1)S(1)}, bf16[4,1,128,256]{3,2,1,0:T(8,128)(2,1)}, u32[]{:S(2)}) copy-start(bf16[4,1,128,256]{3,2,1,0:T(8,128)(2,1)} %param.9) | copy-start | bytes 786436
  490.6 2.0 copy-start.3
  493.5 146.5 %all-reduce.25.cloned.1.call-start = ((), (), s32[]{:S(2)}) async-start(), calls=%async_computation.4 | async-start | bytes 262144 | tf_op jit(solution)/shard_map/psum | solution.py:89
  532.5 323.0 %copy-start.5 = (bf16[4,128,128]{2,1,0:T(8,128)(2,1)S(1)}, bf16[4,128,128]{2,1,0:T(8,128)(2,1)}, u32[]{:S(2)}) copy-start(bf16[4,128,128]{2,1,0:T(8,128)(2,1)} %all-reduce.23.cloned.1.call-done) | copy-start | bytes 393220
  534.4 214.5 %all-reduce.33.cloned.1.call-start = ((), (), s32[]{:S(2)}) async-start(), calls=%async_computation.8 | async-start | bytes 2228224 | tf_op jit(solution)/shard_map/psum | solution.py:9
  535.3 318.0 %all-reduce.27.cloned.1.call-start = ((), (), s32[]{:S(2)}) async-start(), calls=%async_computation.5 | async-start | bytes 262144 | tf_op jit(solution)/shard_map/psum | solution.py:89
  751.0 206.8 %all-reduce.29.cloned.1.call-start = ((), (), s32[]{:S(2)}) async-start(), calls=%async_computation.6 | async-start | bytes 262144 | tf_op jit(solution)/shard_map/psum | solution.py:89
  855.3 206.8 %all-reduce.31.cloned.1.call-start = ((), (), s32[]{:S(2)}) async-start(), calls=%async_computation.7 | async-start | bytes 262144 | tf_op jit(solution)/shard_map/psum | solution.py:89
  855.5 104.2 %copy-start.14 = (bf16[128,256]{1,0:T(8,128)(2,1)S(1)}, bf16[128,256]{1,0:T(8,128)(2,1)}, u32[]{:S(2)}) copy-start(bf16[128,256]{1,0:T(8,128)(2,1)} %get-tuple-element.13) | copy-start | bytes 196612
  1063.1 0.7 copy-start.10
Sparse Core Ops, SparseCore 0:
  16.0 42.5 all-reduce.16
  62.7 107.9 all-reduce.38
  178.3 38.9 all-reduce.18
  221.1 107.9 all-reduce.36
  335.9 38.8 all-reduce.20
  378.8 107.9 all-reduce.34
  493.6 38.8 all-reduce.22
  536.3 103.5 all-reduce.24
  644.0 104.9 all-reduce.32
  752.6 100.6 all-reduce.26
  857.1 100.6 all-reduce.28
  961.4 100.6 all-reduce.30
where the time goes:
time: 1070 us
  waiting for transfers between devices  974 us (91%)
  matrix products  44.8 us (4%)
  between operations  29.6 us (3%)
  local copies, waits for them, and re-layouts  18 us (2%)
    psum x8, waiting for transfers between devices, spread(): return lax.psum(block, axis)  578 us
    psum x4, waiting for transfers between devices, body(): total = lax.psum(partial_sum, 'wide')  396 us
  transfers between devices with their start and end apart: 12, of which 12 were waited for; matrix products, arithmetic and copies ran while one was open for 3% of the time, Pallas kernels for 0%

commit v1 on v0

--- a/solution.py
+++ b/solution.py
@@ -86,7 +86,7 @@
         partial_sum = jnp.einsum(
             "rac,ran->cn", saved_left[section], current, preferred_element_type=jnp.float32
         )
-        total = lax.psum(partial_sum, "wide")
+        total = lax.all_gather(partial_sum, "wide").sum(axis=0)
         corrected = (saved_pivot[section].astype(jnp.float32) - total).astype(jnp.bfloat16)
         result = jnp.einsum(
             "ac,cn->an", pivot_weight(target), corrected, preferred_element_type=jnp.float32

time: 1070 us -> 851 us (0.80)
  waiting for transfers between devices: 974 us -> 750 us
    psum x4 -> x0, waiting for transfers between devices: 396 us -> none  [body(): total = lax.psum(partial_sum, 'wide')]
    all_gather x0 -> x4, waiting for transfers between devices: none -> 173 us  [body(): total = lax.all_gather(partial_sum, 'wide').sum(axis=0)]
where the time goes in v1:
time: 851 us; the launch traced here: 850 us
  waiting for transfers between devices  750 us (88%)
  matrix products  39.7 us (5%)
  between operations  30.3 us (4%)
  local copies, waits for them, and re-layouts  15.8 us (2%)
  other arithmetic  13.4 us (2%)
    psum x8, waiting for transfers between devices, spread(): return lax.psum(block, axis)  577 us
    all_gather x4, waiting for transfers between devices, body(): total = lax.all_gather(partial_sum, 'wide').sum(axis=0)  173 us
  transfers between devices with their start and end apart: 12, of which 12 were waited for; matrix products, arithmetic and copies ran while one was open for 3% of the time, Pallas kernels for 0%

profile of v1, /device:TPU:1, one launch (start us, length us, event | category | flops | bytes accessed | tf_op | source)
XLA Modules:
  0.0 850.2 jit_solution(4111275735584590021)
XLA Ops:
  7.2 1.5 fusion.111
  13.5 1.5 constant_dynamic-slice_fusion.1
  16.0 1.3 constant_dynamic-slice_fusion
  18.0 1.6 fusion.2
  24.7 33.9 %all-reduce.13.cloned.1.call-done = bf16[4,128,128]{2,1,0:T(8,128)(2,1)} async-done(((bf16[4,128,128]{2,1,0:T(8,128)(2,1)}), bf16[4,128,128]{2,1,0:T(8,128)(2,1)}) %all-reduce.13.cloned.1.call-update) | async-done | bytes 131088 | tf_op jit(solution)/shard_map/psum | solution.py:9
  58.6 112.0 %all-reduce.27.cloned.1.call-done = (bf16[128,32,128]{2,0,1:T(8,128)(2,1)}, bf16[128,256]{1,0:T(8,128)(2,1)}) async-done(((bf16[128,32,128]{2,0,1:T(8,128)(2,1)}, bf16[128,256]{1,0:T(8,128)(2,1)}), (bf16[128,32,128]{2,0,1:T(8,128)(2,1)}, bf16[128,256]{1,0:T(8,128)(2,1)})) %all-reduce.27.cloned.1.call-update) | async-done | bytes 1114128 | tf_op jit(solution)/shard_map/psum | solution.py:9
  170.6 4.7 fusion
  175.3 2.0 copy-done.2
  178.2 2.7 fusion.3
  185.9 31.3 %all-reduce.15.cloned.1.call-done = bf16[4,128,128]{2,1,0:T(8,128)(2,1)} async-done(((bf16[4,128,128]{2,1,0:T(8,128)(2,1)}), bf16[4,128,128]{2,1,0:T(8,128)(2,1)}) %all-reduce.15.cloned.1.call-update) | async-done | bytes 131088 | tf_op jit(solution)/shard_map/psum | solution.py:9
  217.2 111.8 %all-reduce.25.cloned.1.call-done = (bf16[128,32,128]{2,0,1:T(8,128)(2,1)}, bf16[128,256]{1,0:T(8,128)(2,1)}) async-done(((bf16[128,32,128]{2,0,1:T(8,128)(2,1)}, bf16[128,256]{1,0:T(8,128)(2,1)}), (bf16[128,32,128]{2,0,1:T(8,128)(2,1)}, bf16[128,256]{1,0:T(8,128)(2,1)})) %all-reduce.25.cloned.1.call-update) | async-done | bytes 1114128 | tf_op jit(solution)/shard_map/psum | solution.py:9
  329.1 3.8 subtract_convert_fusion.2
  332.9 2.0 copy-done.3
  335.8 2.7 fusion.4
  343.5 31.4 %all-reduce.17.cloned.1.call-done = bf16[4,128,128]{2,1,0:T(8,128)(2,1)} async-done(((bf16[4,128,128]{2,1,0:T(8,128)(2,1)}), bf16[4,128,128]{2,1,0:T(8,128)(2,1)}) %all-reduce.17.cloned.1.call-update) | async-done | bytes 131088 | tf_op jit(solution)/shard_map/psum | solution.py:9
  374.9 111.8 %all-reduce.23.cloned.1.call-done = (bf16[128,32,128]{2,0,1:T(8,128)(2,1)}, bf16[128,256]{1,0:T(8,128)(2,1)}) async-done(((bf16[128,32,128]{2,0,1:T(8,128)(2,1)}, bf16[128,256]{1,0:T(8,128)(2,1)}), (bf16[128,32,128]{2,0,1:T(8,128)(2,1)}, bf16[128,256]{1,0:T(8,128)(2,1)})) %all-reduce.23.cloned.1.call-update) | async-done | bytes 1114128 | tf_op jit(solution)/shard_map/psum | solution.py:9
  486.7 3.8 subtract_convert_fusion.1
  490.6 2.0 copy-done.1
  493.5 39.0 %all-reduce.19.cloned.1.call-done = bf16[4,128,128]{2,1,0:T(8,128)(2,1)} async-done(((bf16[4,128,128]{2,1,0:T(8,128)(2,1)}), bf16[4,128,128]{2,1,0:T(8,128)(2,1)}) %all-reduce.19.cloned.1.call-update) | async-done | bytes 131088 | tf_op jit(solution)/shard_map/psum | solution.py:9
  532.5 1.8 convolution_bitcast_fusion.3
  535.5 2.7 fusion.5
  538.9 45.5 %all-gather.9.cloned.1.call-done = f32[4096,256]{1,0:T(8,128)} async-done(((f32[128,256]{1,0:T(8,128)}), f32[4096,256]{1,0:T(8,128)}) %all-gather.9.cloned.1.call-update) | async-done | bytes 4194320 | tf_op jit(solution)/shard_map/all_gather | solution.py:89
  584.4 2.4 reduce_sum.36
  586.9 106.0 %all-reduce.21.cloned.1.call-done = (bf16[128,32,128]{2,0,1:T(8,128)(2,1)}, bf16[128,256]{1,0:T(8,128)(2,1)}) async-done(((bf16[128,32,128]{2,0,1:T(8,128)(2,1)}, bf16[128,256]{1,0:T(8,128)(2,1)}), (bf16[128,32,128]{2,0,1:T(8,128)(2,1)}, bf16[128,256]{1,0:T(8,128)(2,1)})) %all-reduce.21.cloned.1.call-update) | async-done | bytes 1114128 | tf_op jit(solution)/shard_map/psum | solution.py:9
  695.5 46.2 %all-gather.11.cloned.1.call-done = f32[4096,256]{1,0:T(8,128)} async-done(((f32[128,256]{1,0:T(8,128)}), f32[4096,256]{1,0:T(8,128)}) %all-gather.11.cloned.1.call-update) | async-done | bytes 4194320 | tf_op jit(solution)/shard_map/all_gather | solution.py:89
  741.7 2.4 reduce_sum.37
  746.2 44.7 %all-gather.13.cloned.1.call-done = f32[4096,256]{1,0:T(8,128)} async-done(((f32[128,256]{1,0:T(8,128)}), f32[4096,256]{1,0:T(8,128)}) %all-gather.13.cloned.1.call-update) | async-done | bytes 4194320 | tf_op jit(solution)/shard_map/all_gather | solution.py:89
  790.9 2.4 reduce_sum.38
  794.4 3.4 fusion.1
  797.9 4.7 copy.38
  803.5 36.5 %all-gather.15.cloned.1.call-done = f32[4096,256]{1,0:T(8,128)} async-done(((f32[128,256]{1,0:T(8,128)}), f32[4096,256]{1,0:T(8,128)}) %all-gather.15.cloned.1.call-update) | async-done | bytes 4194320 | tf_op jit(solution)/shard_map/all_gather | solution.py:89
  840.0 2.4 reduce_sum.39
  (85 shorter events, 17.7 us)
Async XLA Ops:
  7.2 7.8 copy-start
  7.2 12.5 %copy-start.10 = (bf16[4,1,128,256]{3,2,1,0:T(8,128)(2,1)S(1)}, bf16[4,1,128,256]{3,2,1,0:T(8,128)(2,1)}, u32[]{:S(2)}) copy-start(bf16[4,1,128,256]{3,2,1,0:T(8,128)(2,1)} %param.8) | copy-start | bytes 786436
  7.2 16.8 %copy-start.16 = (s32[4,1,32,1]{2,3,1,0:T(1,128)S(1)}, s32[4,1,32,1]{2,3,1,0:T(1,128)}, u32[]{:S(2)}) copy-start(s32[4,1,32,1]{2,3,1,0:T(1,128)} %param.10) | copy-start | bytes 1540
  7.2 51.4 %all-reduce.13.cloned.1.call-start = ((), (), s32[]{:S(2)}) async-start(), calls=%async_computation | async-start | bytes 262144 | tf_op jit(solution)/shard_map/psum | solution.py:9
  15.9 154.7 %all-reduce.27.cloned.1.call-start = ((), (), s32[]{:S(2)}) async-start(), calls=%async_computation.11 | async-start | bytes 2228224 | tf_op jit(solution)/shard_map/psum | solution.py:9
  20.5 196.7 %all-reduce.15.cloned.1.call-start = ((), (), s32[]{:S(2)}) async-start(), calls=%async_computation.1 | async-start | bytes 262144 | tf_op jit(solution)/shard_map/psum | solution.py:9
  170.6 10.3 %copy-start.8 = (bf16[4,128,128]{2,1,0:T(8,128)(2,1)S(1)}, bf16[4,128,128]{2,1,0:T(8,128)(2,1)}, u32[]{:S(2)}) copy-start(bf16[4,128,128]{2,1,0:T(8,128)(2,1)} %all-reduce.13.cloned.1.call-done) | copy-start | bytes 393220
  170.6 10.3 %copy-start.12 = (bf16[128,256]{1,0:T(8,128)(2,1)S(1)}, bf16[128,256]{1,0:T(8,128)(2,1)}, u32[]{:S(2)}) copy-start(bf16[128,256]{1,0:T(8,128)(2,1)} %get-tuple-element.19) | copy-start | bytes 196612
  175.3 2.0 copy-start.2
  178.2 150.9 %all-reduce.25.cloned.1.call-start = ((), (), s32[]{:S(2)}) async-start(), calls=%async_computation.10 | async-start | bytes 2228224 | tf_op jit(solution)/shard_map/psum | solution.py:9
  182.0 192.9 %all-reduce.17.cloned.1.call-start = ((), (), s32[]{:S(2)}) async-start(), calls=%async_computation.2 | async-start | bytes 262144 | tf_op jit(solution)/shard_map/psum | solution.py:9
  329.1 9.5 %copy-start.9 = (bf16[4,128,128]{2,1,0:T(8,128)(2,1)S(1)}, bf16[4,128,128]{2,1,0:T(8,128)(2,1)}, u32[]{:S(2)}) copy-start(bf16[4,128,128]{2,1,0:T(8,128)(2,1)} %all-reduce.15.cloned.1.call-done) | copy-start | bytes 393220
  329.1 9.5 %copy-start.13 = (bf16[128,256]{1,0:T(8,128)(2,1)S(1)}, bf16[128,256]{1,0:T(8,128)(2,1)}, u32[]{:S(2)}) copy-start(bf16[128,256]{1,0:T(8,128)(2,1)} %get-tuple-element.17) | copy-start | bytes 196612
  332.9 2.0 copy-start.3
  335.8 150.9 %all-reduce.23.cloned.1.call-start = ((), (), s32[]{:S(2)}) async-start(), calls=%async_computation.9 | async-start | bytes 2228224 | tf_op jit(solution)/shard_map/psum | solution.py:9
  339.6 192.9 %all-reduce.19.cloned.1.call-start = ((), (), s32[]{:S(2)}) async-start(), calls=%async_computation.3 | async-start | bytes 262144 | tf_op jit(solution)/shard_map/psum | solution.py:9
  486.7 45.8 %copy-start.6 = (bf16[4,1,128,256]{3,2,1,0:T(8,128)(2,1)S(1)}, bf16[4,1,128,256]{3,2,1,0:T(8,128)(2,1)}, u32[]{:S(2)}) copy-start(bf16[4,1,128,256]{3,2,1,0:T(8,128)(2,1)} %param.9) | copy-start | bytes 786436
  486.7 47.7 %copy-start.4 = (bf16[4,128,128]{2,1,0:T(8,128)(2,1)S(1)}, bf16[4,128,128]{2,1,0:T(8,128)(2,1)}, u32[]{:S(2)}) copy-start(bf16[4,128,128]{2,1,0:T(8,128)(2,1)} %all-reduce.17.cloned.1.call-done) | copy-start | bytes 393220
  486.7 47.7 %copy-start.14 = (bf16[128,256]{1,0:T(8,128)(2,1)S(1)}, bf16[128,256]{1,0:T(8,128)(2,1)}, u32[]{:S(2)}) copy-start(bf16[128,256]{1,0:T(8,128)(2,1)} %get-tuple-element.15) | copy-start | bytes 196612
  490.6 2.0 copy-start.1
  493.4 91.0 %all-gather.9.cloned.1.call-start = ((), (), s32[]{:S(2)}) async-start(), calls=%async_computation.4 | async-start | bytes 4325376 | tf_op jit(solution)/shard_map/all_gather | solution.py:89
  534.3 158.5 %all-reduce.21.cloned.1.call-start = ((), (), s32[]{:S(2)}) async-start(), calls=%async_computation.8 | async-start | bytes 2228224 | tf_op jit(solution)/shard_map/psum | solution.py:9
  538.2 203.5 %all-gather.11.cloned.1.call-start = ((), (), s32[]{:S(2)}) async-start(), calls=%async_computation.5 | async-start | bytes 4325376 | tf_op jit(solution)/shard_map/all_gather | solution.py:89
  694.8 96.1 %all-gather.13.cloned.1.call-start = ((), (), s32[]{:S(2)}) async-start(), calls=%async_computation.6 | async-start | bytes 4325376 | tf_op jit(solution)/shard_map/all_gather | solution.py:89
  744.1 50.3 %copy-start.5 = (bf16[4,128,128]{2,1,0:T(8,128)(2,1)S(1)}, bf16[4,128,128]{2,1,0:T(8,128)(2,1)}, u32[]{:S(2)}) copy-start(bf16[4,128,128]{2,1,0:T(8,128)(2,1)} %all-reduce.19.cloned.1.call-done) | copy-start | bytes 393220
  744.1 50.3 %copy-start.7 = (bf16[128,32,128]{2,0,1:T(8,128)(2,1)S(1)}, bf16[128,32,128]{2,0,1:T(8,128)(2,1)}, u32[]{:S(2)}) copy-start(bf16[128,32,128]{2,0,1:T(8,128)(2,1)} %get-tuple-element.12) | copy-start | bytes 3145732
  745.2 94.8 %all-gather.15.cloned.1.call-start = ((), (), s32[]{:S(2)}) async-start(), calls=%async_computation.7 | async-start | bytes 4325376 | tf_op jit(solution)/shard_map/all_gather | solution.py:89
  797.9 4.7 copy-start.15
  842.6 0.7 copy-start.11
Sparse Core Ops, SparseCore 0:
  16.0 42.5 all-reduce.12
  62.6 107.9 all-reduce.26
  178.3 38.9 all-reduce.14
  221.1 107.9 all-reduce.24
  335.9 38.8 all-reduce.16
  378.7 107.9 all-reduce.22
  493.6 38.8 all-reduce.18
  535.3 49.0 all-gather.8
  588.4 104.3 all-reduce.20
  695.5 46.1 all-gather.10
  745.4 45.4 all-gather.12
  794.5 45.4 all-gather.14
